TPU v7x, 32 devices: a whole 2x2x4 slice. The times are simulated.
32 devices in a mesh: row: 4 (over y, core), col: 8 (over z, x).
Axes of the slice: x: 2, y: 2, z: 4, core: 2. Of those that a mesh axis runs over, the one named last changes fastest.
Arguments:
- hess_inv: float32 [16384, 16384], P('row', 'col'), as said below
- weights: bfloat16 [6144, 16384], P('row', 'col'), may hold values from -6 to 6
- removed: int32 [128], replicated, may hold values from 0 to 16383, as said below
Outputs:
- hess_out: float32 [16384, 16384], P('row', 'col')
- weight_out: bfloat16 [6144, 16384], P('row', 'col')
Inputs may be any that keep to these rules, and one draw needn't show every extreme that they name: `removed`: sorted ascending and distinct; each aligned block of 2048 columns holds at most 48 of them, and at least one block holds exactly 48. `hess_inv`: symmetric and positive definite.
All inputs are finite; a program needn't handle non-finite values.
Results may differ from a plain program's by a relative error of at most 0.005.
Values may be sent and summed in bfloat16 or wider, within the bound.
No kernel may reach another device: no remote copies, remote signals or barrier semaphores. Data moves between devices by JAX's collectives and lax.ppermute only.
A program may use at most 128 MiB of HBM per device.

v0:
```python
import jax
import jax.numpy as jnp
from jax import lax
from jax.sharding import PartitionSpec as P

MOST = 48


def spread(block, axis, owner):
    block = jnp.where(lax.axis_index(axis) == owner, block, jnp.zeros_like(block))
    return lax.psum(block, axis)


def pick_owned(source, removed, tile_index, tile_size, slot_count, which_axis):
    before = jnp.sum((removed < tile_index * tile_size).astype(jnp.int32))
    within = jnp.sum((removed // tile_size == tile_index).astype(jnp.int32))
    slot_rank = jnp.arange(slot_count, dtype=jnp.int32)
    chosen = jnp.clip(before + slot_rank, 0, removed.shape[0] - 1)
    local_col = jnp.clip(removed[chosen] - tile_index * tile_size, 0, tile_size - 1)
    taken_part = jnp.take(source, local_col, axis=which_axis)
    live_slot = slot_rank < within
    mask_shape = [1, 1]
    mask_shape[which_axis] = slot_count
    return jnp.where(live_slot.reshape(mask_shape), taken_part, jnp.zeros((), taken_part.dtype))


def slot_map(removed, tile_size, slot_count):
    which_tile = removed // tile_size
    first_pos = jnp.sum(
        (removed[None, :] < (which_tile * tile_size)[:, None]).astype(jnp.int32), axis=1
    )
    position = jnp.arange(removed.shape[0], dtype=jnp.int32)
    return which_tile * slot_count + position - first_pos


def on_device(hess_inv, weights, removed):
    row_count = lax.axis_size("row")
    col_count = lax.axis_size("col")
    row_index = lax.axis_index("row")
    col_index = lax.axis_index("col")
    row_tile, col_tile = hess_inv.shape
    tile_ratio = col_count // row_count
    col_slots = slot_map(removed, col_tile, MOST)
    packed_weight = pick_owned(weights, removed, col_index, col_tile, MOST, 1)
    packed_rows = pick_owned(hess_inv, removed, row_index, row_tile, tile_ratio * MOST, 0)
    gathered = lax.all_gather(packed_rows, "row", axis=0, tiled=True)
    upper_rows = jnp.take(gathered, slot_map(removed, row_tile, tile_ratio * MOST), axis=0)
    pieces = [
        spread(upper_rows.astype(jnp.bfloat16), "col", row_index * tile_ratio + offset).astype(
            upper_rows.dtype
        )
        for offset in range(tile_ratio)
    ]
    left_rows = jnp.concatenate(pieces, axis=1)
    weight_wide = lax.all_gather(packed_weight, "col", axis=1, tiled=True)
    weight_left = jnp.take(weight_wide, col_slots, axis=1)
    own_cols = pick_owned(upper_rows, removed, col_index, col_tile, MOST, 1)
    block_wide = lax.all_gather(own_cols, "col", axis=1, tiled=True)
    removed_block = jnp.take(block_wide, col_slots, axis=1)
    factor = jnp.linalg.cholesky(removed_block)
    identity = jnp.eye(removed_block.shape[0], dtype=jnp.float32)
    factor_inv = jax.scipy.linalg.solve_triangular(factor, identity, lower=True)
    block_inv = jnp.dot(factor_inv.T, factor_inv, precision=lax.Precision.HIGHEST)
    coupling = jnp.dot(block_inv, upper_rows, precision=lax.Precision.HIGHEST)
    correction = lax.dot_general(
        left_rows, coupling, (((0,), (0,)), ((), ())), precision=lax.Precision.HIGHEST
    )
    hess_out = hess_inv - correction
    weight_fix = jnp.dot(weight_left.astype(jnp.float32), coupling, precision=lax.Precision.HIGHEST)
    weight_out = (weights.astype(jnp.float32) - weight_fix).astype(jnp.bfloat16)
    return (hess_out, weight_out)


def solution(mesh):
    placed = (P("row", "col"), P("row", "col"), P())
    return jax.shard_map(
        on_device,
        mesh=mesh,
        in_specs=placed,
        out_specs=(P("row", "col"), P("row", "col")),
        check_vma=False,
    )
```

profile of v0, /device:TPU:0, one launch (start us, length us, event | category | flops | bytes accessed | tf_op | source)
XLA Modules:
  0.0 271.6 jit_solution(3088426548601150920)
XLA Ops:
  7.2 0.0 all-gather.5.cloned.1.call-start
  7.2 1.4 fusion.12
  8.6 0.7 fusion.16
  9.3 1.4 gather_fusion.3
  10.8 0.7 iota_compare_fusion.3
  11.4 0.0 copy-start
  11.4 8.6 %copy.13 = bf16[1536,2048]{0,1:T(8,128)(2,1)} copy(bf16[1536,2048]{1,0:T(8,128)(2,1)} %param.4) | data formatting | bytes 12582912 | tf_op args[1]
  20.0 4.4 %gather_fusion.6 = bf16[48,1536]{1,0:T(8,128)(2,1)S(1)} fusion(bf16[1536,2048]{0,1:T(8,128)(2,1)} %copy.13, s32[1024]{0:T(1024)S(1)} %pad_clamp_fusion.1), kind=kCustom, calls=%fused_computation.6 | custom fusion | bytes 295104 | tf_op jit(solution)/shard_map/jit(_take)/gather | solution.py:20
  24.4 0.8 select_bitcast_fusion
  25.2 0.0 all-gather.5.cloned.1.call-update
  25.2 0.0 all-gather.3.cloned.1.call-start
  25.3 0.7 fusion.14
  26.0 0.0 copy-done
  26.0 1.2 gather_fusion
  27.3 11.9 %gather_fusion.1 = f32[96,2048]{1,0:T(8,128)S(1)} fusion(f32[4096,2048]{1,0:T(8,128)} %param.3, s32[1024]{0:T(1024)S(1)} %pad_clamp_fusion.4), kind=kCustom, calls=%fused_computation.1 | custom fusion | bytes 1573248 | tf_op jit(solution)/shard_map/jit(_take)/gather | solution.py:20
  39.2 0.6 fusion.10
  39.8 0.6 iota_compare_fusion.4
  40.5 1.0 select_select_fusion
  41.5 0.0 all-gather.3.cloned.1.call-update
  41.6 0.0 all-reduce.3.cloned.1.call-start
  41.6 0.2 convert_reduce_fusion
  41.9 27.4 %all-gather.5.cloned.1.call-done = bf16[1536,384]{0,1:T(8,128)(2,1)} async-done(((bf16[1536,48]{0,1:T(8,128)(2,1)}), bf16[1536,384]{0,1:T(8,128)(2,1)}) %all-gather.5.cloned.1.call-update) | async-done | bytes 1179664 | tf_op jit(solution)/shard_map/all_gather | solution.py:55
  69.2 2.7 gather_fusion.7
  71.9 26.7 %all-gather.3.cloned.1.call-done = f32[384,2048]{1,0:T(8,128)} async-done(((f32[96,2048]{1,0:T(8,128)}), f32[384,2048]{1,0:T(8,128)}) %all-gather.3.cloned.1.call-update) | async-done | bytes 3145744 | tf_op jit(solution)/shard_map/all_gather | solution.py:46
  98.6 3.3 %gather_fusion.2 = f32[128,2048]{1,0:T(8,128)S(1)} fusion(f32[384,2048]{1,0:T(8,128)} %all-gather.3.cloned.1.call-done, s32[1024]{0:T(1024)S(1)} %pad_clamp_fusion.3), kind=kCustom, calls=%fused_computation.2 | custom fusion | bytes 2097664 | tf_op jit(solution)/shard_map/jit(_take)/gather | solution.py:47
  101.9 1.0 broadcast_select_fusion.2
  102.9 0.3 copy.11
  103.2 0.9 broadcast_select_fusion.1
  104.1 0.6 gather_fusion.4
  104.7 0.1 select_bitcast_fusion.1
  104.8 30.9 %all_gather.10 = f32[128,384]{0,1:T(8,128)S(1)} all-gather(f32[128,48]{0,1:T(8,128)S(1)} %select_bitcast_fusion.1), channel_id=1, replica_groups=mesh['row'=4,'col'=8] {'col'}, dimensions={1}, use_global_device_ids=true | all-gather | bytes 221184 | tf_op jit(solution)/shard_map/all_gather | solution.py:58
  135.7 0.6 gather_fusion.5
  136.3 0.1 broadcast_select_fusion.3
  136.4 0.1 copy.12
  136.5 0.1 fusion.9
  136.6 11.7 %cholesky.16 = f32[128,128]{1,0:T(8,128)S(1)} custom-call(f32[128,128]{1,0:T(8,128)S(1)} %fusion.9), custom_call_target="Cholesky" | custom-call | tf_op jit(solution)/shard_map/jit(cholesky)/cholesky | solution.py:60
  148.3 0.6 compare_reduce_fusion
  149.0 0.7 fusion.6
  149.6 9.8 %custom-call.7 = f32[1,128,128]{1,2,0:T(8,128)S(1)} custom-call(f32[1,128,128]{2,1,0:T(8,128)S(1)} %fusion.6), custom_call_target="InvertDiagBlocksLowerTriangular" | custom-call | tf_op jit(solution)/shard_map/jit(_solve_triangular)/triangular_solve | solution.py:62
  159.5 0.3 fusion.7
  159.7 0.0 all-reduce.3.cloned.1.call-update
  159.7 0.3 fusion.20
  160.0 1.0 fusion.21
  161.0 9.6 %subtract_convert_fusion = bf16[1536,2048]{1,0:T(8,128)(2,1)} fusion(bf16[1536,2048]{1,0:T(8,128)(2,1)} %param.4, f32[128,2048]{1,0:T(8,128)S(1)} %fusion.21, bf16[128,1536]{1,0:T(8,128)(2,1)S(1)} %gather_fusion.7, pred[128]{0:T(512)(128)(4,1)S(1)} %get-tuple-element.10), kind=kOutput, calls=%fused_computation.9 | convolution fusion | flops 4841472000 | bytes 14024832 | tf_op jit(solution)/shard_map/dot_general | solution.py:69
  170.6 67.6 %all-reduce.3.cloned.1.call-done = (bf16[128,2048]{1,0:T(8,128)(2,1)}, bf16[128,2048]{1,0:T(8,128)(2,1)}) async-done(((bf16[128,2048]{1,0:T(8,128)(2,1)}, bf16[128,2048]{1,0:T(8,128)(2,1)}), (bf16[128,2048]{1,0:T(8,128)(2,1)}, bf16[128,2048]{1,0:T(8,128)(2,1)})) %all-reduce.3.cloned.1.call-update) | async-done | bytes 1048592 | tf_op jit(solution)/shard_map/psum | solution.py:11
  238.2 26.9 %convolution_subtract_fusion = f32[4096,2048]{1,0:T(8,128)} fusion(f32[4096,2048]{1,0:T(8,128)} %param.3, f32[128,2048]{1,0:T(8,128)S(1)} %fusion.21, bf16[128,2048]{1,0:T(8,128)(2,1)} %get-tuple-element.6, bf16[128,2048]{1,0:T(8,128)(2,1)} %get-tuple-element.7), kind=kOutput, calls=%fused_computation.8 | convolution fusion | flops 12895387648 | bytes 69206016 | tf_op jit(solution)/shard_map/dot_general | solution.py:65
  (13 shorter events, 0.1 us)
Async XLA Ops:
  7.2 62.1 %all-gather.5.cloned.1.call-start = ((), (), s32[]{:S(2)}) async-start(), calls=%async_computation.1 | async-start | bytes 1327104 | tf_op jit(solution)/shard_map/all_gather | solution.py:55
  11.4 14.6 %copy-start = (s32[128]{0:T(128)S(1)}, s32[128]{0:T(128)}, u32[]{:S(2)}) copy-start(s32[128]{0:T(128)} %param.5) | copy-start | bytes 1540
  25.2 73.4 %all-gather.3.cloned.1.call-start = ((), (), s32[]{:S(2)}) async-start(), calls=%async_computation | async-start | bytes 3932160 | tf_op jit(solution)/shard_map/all_gather | solution.py:46
  41.6 196.6 %all-reduce.3.cloned.1.call-start = ((), (), s32[]{:S(2)}) async-start(), calls=%async_computation.2 | async-start | bytes 2097152 | tf_op jit(solution)/shard_map/psum | solution.py:11
Sparse Core Ops, SparseCore 0:
  25.3 43.8 all-gather.4
  71.4 27.1 all-gather.2
  159.9 78.2 all-reduce.2
where the time goes:
time: 272 us
  waiting for transfers between devices  122 us (45%)
  matrix products  38 us (14%)
  local copies, waits for them, and re-layouts  35.3 us (13%)
  other arithmetic  31.7 us (12%)
  blocking collectives  30.9 us (11%)
  between operations  14 us (5%)
    psum x1, waiting for transfers between devices, spread(): return lax.psum(block, axis)  67.6 us
    all_gather x1, blocking collectives, on_device(): block_wide = lax.all_gather(own_cols, 'col', axis=1, tiled=True)  30.9 us
    all_gather x1, waiting for transfers between devices, on_device(): weight_wide = lax.all_gather(packed_weight, 'col', axis=1, tiled=True)  27.4 us
    dot_general x1, matrix products, on_device(): lax.dot_general(left_rows, coupling, (((0,), (0,)), ((), ())), precision=...  26.9 us
    all_gather x1, waiting for transfers between devices, on_device(): gathered = lax.all_gather(packed_rows, 'row', axis=0, tiled=True)  26.7 us
    gather x3, local copies, waits for them, and re-layouts, pick_owned(): taken_part = jnp.take(source, local_col, axis=which_axis)  16.9 us
    another operation x3, other arithmetic, on_device(): factor = jnp.linalg.cholesky(removed_block)  12.4 us
    another operation x2, other arithmetic, on_device(): factor_inv = jax.scipy.linalg.solve_triangular(factor, identity, lower=True)  10.5 us
  transfers between devices with their start and end apart: 3, of which 3 were waited for; matrix products, arithmetic and copies ran while one was open for 11% of the time, Pallas kernels for 0%

commit v1 on v0

--- a/solution.py
+++ b/solution.py
@@ -55,7 +55,19 @@
     weight_wide = lax.all_gather(packed_weight, "col", axis=1, tiled=True)
     weight_left = jnp.take(weight_wide, col_slots, axis=1)
     own_cols = pick_owned(upper_rows, removed, col_index, col_tile, MOST, 1)
-    block_wide = lax.all_gather(own_cols, "col", axis=1, tiled=True)
+    ndev = jax.lax.axis_size("col")
+    pile = [(k, (k + 1) % ndev) for k in range(ndev)]
+    w1, long_array = ([own_cols], [own_cols])
+    history = [(k, (k - 1) % ndev) for k in range(ndev)]
+    for _ in range(ndev // 2):
+        outer = jax.lax.ppermute(w1[-1], "col", pile)
+        w1.append(outer)
+    for _ in range((ndev - 1) // 2):
+        part_next = jax.lax.ppermute(long_array[-1], "col", history)
+        long_array.append(part_next)
+    later = jnp.concatenate([*w1[::-1], *long_array[1:]], axis=1)
+    f_now = jax.lax.axis_index("col")
+    block_wide = jnp.roll(later, (f_now - ndev // 2) * own_cols.shape[1], axis=1)
     removed_block = jnp.take(block_wide, col_slots, axis=1)
     factor = jnp.linalg.cholesky(removed_block)
     identity = jnp.eye(removed_block.shape[0], dtype=jnp.float32)

time: 272 us -> 223 us (0.82)
  waiting for transfers between devices: 122 us -> 88.8 us
  blocking collectives: 30.9 us -> 0 us
  starting transfers between devices: 0.12 us -> 13.2 us
    all_gather x1 -> x0, blocking collectives: 30.9 us -> none  [on_device(): block_wide = lax.all_gather(own_cols, 'col', axis=1, tiled=True)]
    psum x1, waiting for transfers between devices: 67.6 us -> 37.8 us  [spread(): return lax.psum(block, axis)]
    ppermute x0 -> x7, starting transfers between devices: none -> 13.1 us  [the longest x3 11.5 us: on_device(): part_next = jax.lax.ppermute(long_array[-1], 'col', history)]
    all_gather x1, waiting for transfers between devices: 26.7 us -> 16 us  [on_device(): gathered = lax.all_gather(packed_rows, 'row', axis=0, tiled=True)]
    ppermute x0 -> x7, waiting for transfers between devices: none -> 9.18 us  [the longest x4 6.91 us: on_device(): outer = jax.lax.ppermute(w1[-1], 'col', pile)]
    unnamed x3 -> x16, local copies, waits for them, and re-layouts: 8.62 us -> 8.67 us
  transfers between devices with their start and end apart: 3 -> 10, of which waited for: 3 -> 7; matrix products, arithmetic and copies ran while one was open for 11% -> 27% of each run, Pallas kernels for 0% -> 0%
where the time goes in v1:
time: 223 us; the launch traced here: 222 us
  waiting for transfers between devices  88.8 us (40%)
  matrix products  38 us (17%)
  local copies, waits for them, and re-layouts  36.2 us (16%)
  other arithmetic  31.7 us (14%)
  between operations  14.1 us (6%)
  starting transfers between devices  13.2 us (6%)
    psum x1, waiting for transfers between devices, spread(): return lax.psum(block, axis)  37.8 us
    dot_general x1, matrix products, on_device(): lax.dot_general(left_rows, coupling, (((0,), (0,)), ((), ())), precision=...  26.9 us
    all_gather x1, waiting for transfers between devices, on_device(): weight_wide = lax.all_gather(packed_weight, 'col', axis=1, tiled=True)  25.8 us
    gather x3, local copies, waits for them, and re-layouts, pick_owned(): taken_part = jnp.take(source, local_col, axis=which_axis)  17.4 us
    all_gather x1, waiting for transfers between devices, on_device(): gathered = lax.all_gather(packed_rows, 'row', axis=0, tiled=True)  16 us
    another operation x3, other arithmetic, on_device(): factor = jnp.linalg.cholesky(removed_block)  12.4 us
    ppermute x3, starting transfers between devices, on_device(): part_next = jax.lax.ppermute(long_array[-1], 'col', history)  11.5 us
    another operation x2, other arithmetic, on_device(): factor_inv = jax.scipy.linalg.solve_triangular(factor, identity, lower=True)  10.5 us
  transfers between devices with their start and end apart: 10, of which 7 were waited for; matrix products, arithmetic and copies ran while one was open for 27% of the time, Pallas kernels for 0%

profile of v1, /device:TPU:0, one launch (start us, length us, event | category | flops | bytes accessed | tf_op | source)
XLA Modules:
  0.0 222.0 jit_solution(3103524658662190716)
XLA Ops:
  7.2 0.0 all-gather.3.cloned.1.call-start
  7.2 1.3 fusion.12
  8.6 0.7 fusion.14
  9.2 1.6 gather_fusion
  10.8 0.7 fusion.16
  11.5 1.4 gather_fusion.3
  13.0 0.6 fusion.10
  13.6 0.6 iota_compare_fusion.4
  14.3 11.8 %gather_fusion.1 = f32[96,2048]{1,0:T(8,128)S(1)} fusion(f32[4096,2048]{1,0:T(8,128)} %param.3, s32[1024]{0:T(1024)S(1)} %get-tuple-element.25), kind=kCustom, calls=%fused_computation.1 | custom fusion | bytes 1573248 | tf_op jit(solution)/shard_map/jit(_take)/gather | solution.py:20
  26.0 1.0 select_select_fusion
  27.1 0.0 all-gather.3.cloned.1.call-update
  27.1 0.0 copy-start
  27.1 0.0 all-gather.5.cloned.1.call-start
  27.2 8.6 %copy.13 = bf16[1536,2048]{0,1:T(8,128)(2,1)} copy(bf16[1536,2048]{1,0:T(8,128)(2,1)} %param.4) | data formatting | bytes 12582912 | tf_op args[1]
  35.8 5.1 %gather_fusion.6 = bf16[48,1536]{1,0:T(8,128)(2,1)S(1)} fusion(bf16[1536,2048]{0,1:T(8,128)(2,1)} %copy.13, s32[1024]{0:T(1024)S(1)} %get-tuple-element.24), kind=kCustom, calls=%fused_computation.6 | custom fusion | bytes 295104 | tf_op jit(solution)/shard_map/jit(_take)/gather | solution.py:20
  40.9 0.5 iota_compare_fusion.3
  41.4 0.8 select_bitcast_fusion
  42.2 0.0 all-gather.5.cloned.1.call-update
  42.2 0.0 all-reduce.3.cloned.1.call-start
  42.3 0.0 copy-done
  42.3 0.2 convert_reduce_fusion
  42.5 16.0 %all-gather.3.cloned.1.call-done = f32[384,2048]{1,0:T(8,128)} async-done(((f32[96,2048]{1,0:T(8,128)}), f32[384,2048]{1,0:T(8,128)}) %all-gather.3.cloned.1.call-update) | async-done | bytes 3145744 | tf_op jit(solution)/shard_map/all_gather | solution.py:46
  58.5 3.3 %gather_fusion.2 = f32[128,2048]{1,0:T(8,128)S(1)} fusion(f32[384,2048]{1,0:T(8,128)} %all-gather.3.cloned.1.call-done, s32[1024]{0:T(1024)S(1)} %pad_clamp_fusion.3), kind=kCustom, calls=%fused_computation.2 | custom fusion | bytes 2097664 | tf_op jit(solution)/shard_map/jit(_take)/gather | solution.py:47
  61.8 1.0 broadcast_select_fusion.2
  62.8 0.3 copy.11
  63.2 0.6 gather_fusion.4
  63.7 0.1 select_bitcast_fusion.1
  63.8 1.5 collective-permute-start
  65.3 5.1 %collective-permute-done = f32[128,48]{0,1:T(8,128)S(1)} collective-permute-done((f32[128,48]{0,1:T(8,128)S(1)}, f32[128,48]{0,1:T(8,128)S(1)}, u32[]{:S(2)}, u32[]{:S(2)}) %collective-permute-start) | collective-permute-done | bytes 24608 | tf_op jit(solution)/shard_map/ppermute | solution.py:63
  70.4 0.0 collective-permute-start.1
  70.4 4.8 %collective-permute-start.4 = (f32[128,48]{0,1:T(8,128)S(1)}, f32[128,48]{0,1:T(8,128)S(1)}, u32[]{:S(2)}, u32[]{:S(2)}) collective-permute-start(f32[128,48]{0,1:T(8,128)S(1)} %select_bitcast_fusion.1), channel_id=1, source_target_pairs={{0,7},{1,0},{2,1},{3,2},{4,3},{5,4},{6,5},{7,6},{8,15},{9,8},{10,9... | collective-permute-start | bytes 73736 | tf_op jit(solution)/shard_map/ppermute | solution.py:66
  75.2 1.8 collective-permute-done.1
  77.0 0.0 collective-permute-start.2
  77.1 25.8 %all-gather.5.cloned.1.call-done = bf16[1536,384]{0,1:T(8,128)(2,1)} async-done(((bf16[1536,48]{0,1:T(8,128)(2,1)}), bf16[1536,384]{0,1:T(8,128)(2,1)}) %all-gather.5.cloned.1.call-update) | async-done | bytes 1179664 | tf_op jit(solution)/shard_map/all_gather | solution.py:55
  102.9 2.7 %gather_fusion.7 = bf16[128,1536]{1,0:T(8,128)(2,1)S(1)} fusion(bf16[1536,384]{0,1:T(8,128)(2,1)} %all-gather.5.cloned.1.call-done, s32[1024]{0:T(1024)S(1)} %pad_clamp_fusion), kind=kCustom, calls=%fused_computation.7 | custom fusion | bytes 786944 | tf_op jit(solution)/shard_map/jit(_take)/gather | solution.py:56
  105.6 0.0 collective-permute-done.4
  105.6 2.1 collective-permute-start.5
  107.7 0.0 collective-permute-done.2
  107.7 0.0 collective-permute-start.3
  107.7 0.9 broadcast_select_fusion.1
  108.5 0.0 all-reduce.3.cloned.1.call-update
  108.6 0.9 collective-permute-done.5
  109.5 4.7 %collective-permute-start.6 = (f32[128,48]{0,1:T(8,128)S(1)}, f32[128,48]{0,1:T(8,128)S(1)}, u32[]{:S(2)}, u32[]{:S(2)}) collective-permute-start(f32[128,48]{0,1:T(8,128)S(1)} %collective-permute-done.5), channel_id=1, source_target_pairs={{0,7},{1,0},{2,1},{3,2},{4,3},{5,4},{6,5},{7,6},{8,15},{9,8},{10,9... | collective-permute-start | bytes 73736 | tf_op jit(solution)/shard_map/ppermute | solution.py:66
  114.2 0.0 collective-permute-done.3
  114.2 0.1 constant_dynamic-update-slice_fusion.11
  114.3 1.4 collective-permute-done.6
  115.7 0.1 constant_dynamic-update-slice_fusion.3
  115.9 0.6 gather_fusion.5
  116.5 0.1 broadcast_select_fusion.3
  116.6 0.1 copy.12
  116.7 0.1 fusion.9
  116.8 11.7 %cholesky.16 = f32[128,128]{1,0:T(8,128)S(1)} custom-call(f32[128,128]{1,0:T(8,128)S(1)} %fusion.9), custom_call_target="Cholesky" | custom-call | tf_op jit(solution)/shard_map/jit(cholesky)/cholesky | solution.py:72
  128.6 0.6 compare_reduce_fusion
  129.2 0.7 fusion.6
  129.9 9.8 %custom-call.7 = f32[1,128,128]{1,2,0:T(8,128)S(1)} custom-call(f32[1,128,128]{2,1,0:T(8,128)S(1)} %fusion.6), custom_call_target="InvertDiagBlocksLowerTriangular" | custom-call | tf_op jit(solution)/shard_map/jit(_solve_triangular)/triangular_solve | solution.py:74
  139.7 0.2 fusion.7
  139.9 0.3 fusion.20
  140.2 1.0 fusion.21
  141.3 9.6 %subtract_convert_fusion = bf16[1536,2048]{1,0:T(8,128)(2,1)} fusion(bf16[1536,2048]{1,0:T(8,128)(2,1)} %param.4, f32[128,2048]{1,0:T(8,128)S(1)} %fusion.21, bf16[128,1536]{1,0:T(8,128)(2,1)S(1)} %gather_fusion.7, pred[128]{0:T(512)(128)(4,1)S(1)} %get-tuple-element.10), kind=kOutput, calls=%fused_computation.9 | convolution fusion | flops 4841472000 | bytes 14024832 | tf_op jit(solution)/shard_map/dot_general | solution.py:81
  150.8 37.8 %all-reduce.3.cloned.1.call-done = (bf16[128,2048]{1,0:T(8,128)(2,1)}, bf16[128,2048]{1,0:T(8,128)(2,1)}) async-done(((bf16[128,2048]{1,0:T(8,128)(2,1)}, bf16[128,2048]{1,0:T(8,128)(2,1)}), (bf16[128,2048]{1,0:T(8,128)(2,1)}, bf16[128,2048]{1,0:T(8,128)(2,1)})) %all-reduce.3.cloned.1.call-update) | async-done | bytes 1048592 | tf_op jit(solution)/shard_map/psum | solution.py:11
  188.6 26.9 %convolution_subtract_fusion = f32[4096,2048]{1,0:T(8,128)} fusion(f32[4096,2048]{1,0:T(8,128)} %param.3, f32[128,2048]{1,0:T(8,128)S(1)} %fusion.21, bf16[128,2048]{1,0:T(8,128)(2,1)} %get-tuple-element.6, bf16[128,2048]{1,0:T(8,128)(2,1)} %get-tuple-element.7), kind=kOutput, calls=%fused_computation.8 | convolution fusion | flops 12895387648 | bytes 69206016 | tf_op jit(solution)/shard_map/dot_general | solution.py:77
  (27 shorter events, 0.2 us)
Async XLA Ops:
  7.2 51.3 %all-gather.3.cloned.1.call-start = ((), (), s32[]{:S(2)}) async-start(), calls=%async_computation | async-start | bytes 3932160 | tf_op jit(solution)/shard_map/all_gather | solution.py:46
  27.1 15.2 %copy-start = (s32[128]{0:T(128)S(1)}, s32[128]{0:T(128)}, u32[]{:S(2)}) copy-start(s32[128]{0:T(128)} %param.5) | copy-start | bytes 1540
  27.1 75.8 %all-gather.5.cloned.1.call-start = ((), (), s32[]{:S(2)}) async-start(), calls=%async_computation.1 | async-start | bytes 1327104 | tf_op jit(solution)/shard_map/all_gather | solution.py:55
  42.2 146.4 %all-reduce.3.cloned.1.call-start = ((), (), s32[]{:S(2)}) async-start(), calls=%async_computation.2 | async-start | bytes 2097152 | tf_op jit(solution)/shard_map/psum | solution.py:11
  63.8 6.6 %collective-permute-start = (f32[128,48]{0,1:T(8,128)S(1)}, f32[128,48]{0,1:T(8,128)S(1)}, u32[]{:S(2)}, u32[]{:S(2)}) collective-permute-start(f32[128,48]{0,1:T(8,128)S(1)} %select_bitcast_fusion.1), channel_id=1, source_target_pairs={{0,1},{1,2},{2,3},{3,4},{4,5},{5,6},{6,7},{7,0},{8,9},{9,10},{10,1... | collective-permute-start | bytes 73736 | tf_op jit(solution)/shard_map/ppermute | solution.py:63
  70.4 6.6 %collective-permute-start.1 = (f32[128,48]{0,1:T(8,128)S(1)}, f32[128,48]{0,1:T(8,128)S(1)}, u32[]{:S(2)}, u32[]{:S(2)}) collective-permute-start(f32[128,48]{0,1:T(8,128)S(1)} %collective-permute-done), channel_id=1, source_target_pairs={{0,1},{1,2},{2,3},{3,4},{4,5},{5,6},{6,7},{7,0},{8,9},{9,10},{10,1... | collective-permute-start | bytes 73736 | tf_op jit(solution)/shard_map/ppermute | solution.py:63
  70.4 35.2 %collective-permute-start.4 = (f32[128,48]{0,1:T(8,128)S(1)}, f32[128,48]{0,1:T(8,128)S(1)}, u32[]{:S(2)}, u32[]{:S(2)}) collective-permute-start(f32[128,48]{0,1:T(8,128)S(1)} %select_bitcast_fusion.1), channel_id=1, source_target_pairs={{0,7},{1,0},{2,1},{3,2},{4,3},{5,4},{6,5},{7,6},{8,15},{9,8},{10,9... | collective-permute-start | bytes 73736 | tf_op jit(solution)/shard_map/ppermute | solution.py:66
  77.0 30.6 %collective-permute-start.2 = (f32[128,48]{0,1:T(8,128)S(1)}, f32[128,48]{0,1:T(8,128)S(1)}, u32[]{:S(2)}, u32[]{:S(2)}) collective-permute-start(f32[128,48]{0,1:T(8,128)S(1)} %collective-permute-done.1), channel_id=1, source_target_pairs={{0,1},{1,2},{2,3},{3,4},{4,5},{5,6},{6,7},{7,0},{8,9},{9,10},{10,1... | collective-permute-start | bytes 73736 | tf_op jit(solution)/shard_map/ppermute | solution.py:63
  105.6 3.9 %collective-permute-start.5 = (f32[128,48]{0,1:T(8,128)S(1)}, f32[128,48]{0,1:T(8,128)S(1)}, u32[]{:S(2)}, u32[]{:S(2)}) collective-permute-start(f32[128,48]{0,1:T(8,128)S(1)} %collective-permute-done.4), channel_id=1, source_target_pairs={{0,7},{1,0},{2,1},{3,2},{4,3},{5,4},{6,5},{7,6},{8,15},{9,8},{10,9... | collective-permute-start | bytes 73736 | tf_op jit(solution)/shard_map/ppermute | solution.py:66
  107.7 6.5 %collective-permute-start.3 = (f32[128,48]{0,1:T(8,128)S(1)}, f32[128,48]{0,1:T(8,128)S(1)}, u32[]{:S(2)}, u32[]{:S(2)}) collective-permute-start(f32[128,48]{0,1:T(8,128)S(1)} %collective-permute-done.2), channel_id=1, source_target_pairs={{0,1},{1,2},{2,3},{3,4},{4,5},{5,6},{6,7},{7,0},{8,9},{9,10},{10,1... | collective-permute-start | bytes 73736 | tf_op jit(solution)/shard_map/ppermute | solution.py:63
  109.5 6.2 %collective-permute-start.6 = (f32[128,48]{0,1:T(8,128)S(1)}, f32[128,48]{0,1:T(8,128)S(1)}, u32[]{:S(2)}, u32[]{:S(2)}) collective-permute-start(f32[128,48]{0,1:T(8,128)S(1)} %collective-permute-done.5), channel_id=1, source_target_pairs={{0,7},{1,0},{2,1},{3,2},{4,3},{5,4},{6,5},{7,6},{8,15},{9,8},{10,9... | collective-permute-start | bytes 73736 | tf_op jit(solution)/shard_map/ppermute | solution.py:66
Sparse Core Ops, SparseCore 0:
  27.2 31.2 all-gather.2
  61.3 41.5 all-gather.4
  108.7 79.8 all-reduce.2
